TPU v7x, 128 devices: a whole 4x4x4 slice. The times are simulated.
128 devices in a mesh: dp: 8 (over y, core), ctx: 16 (over z, x).
Axes of the slice: x: 4, y: 4, z: 4, core: 2. Of those that a mesh axis runs over, the one named last changes fastest.
Arguments:
- queries: bfloat16 [8, 4096, 256], P('dp', 'ctx'), may hold values from -6 to 6
- keys: bfloat16 [8, 4096, 256], P('dp', 'ctx'), may hold values from -6 to 6
- values: bfloat16 [8, 4096, 256], P('dp', 'ctx'), may hold values from -6 to 6
- grad_out: bfloat16 [8, 4096, 256], P('dp', 'ctx'), may hold values from -6 to 6
- log_norm: float32 [8, 2, 4096], P('dp', None, 'ctx'), may hold values from 5 to 7
- offsets: int32 [2, 5], replicated, may hold values from 0 to 15
- q_gain: float32 [256], replicated, may hold values from 0.5 to 2
Outputs:
- grad_queries: bfloat16 [8, 4096, 256], P('dp', 'ctx')
- grad_keys: bfloat16 [8, 4096, 256], P('dp', 'ctx')
- grad_values: bfloat16 [8, 4096, 256], P('dp', 'ctx')
- grad_gain: float32 [256], replicated
All inputs are finite; a program needn't handle non-finite values.
Results may differ from a plain program's by a relative error of at most 0.013.
The roundings to bfloat16 on the way count: a program that leaves them out, or rounds other values in their place, can miss the bound.
Values may be sent and summed in bfloat16 or wider, within the bound.
No kernel may reach another device: no remote copies, remote signals or barrier semaphores. Data moves between devices by JAX's collectives and lax.ppermute only.
A program may use at most 64 MiB of HBM per device.

v0:
```python
import math
import jax
import jax.numpy as jnp
from jax import lax
from jax.sharding import PartitionSpec as P

BLOCK = 128
LEVELS = 5


def swapped(block, axis, stride):
    count = lax.axis_size(axis)
    route = []
    for low in range(count):
        high = low | 1 << stride
        if high != low and high < count:
            route += [(low, high), (high, low)]
    return lax.ppermute(block, axis, route)


def slot_table(device_local, offset_vec, stride, block_count):
    slot_count = (block_count + stride - 1) // stride
    base_block = device_local * block_count + jnp.zeros_like(offset_vec)
    first_step = jnp.maximum((base_block - offset_vec + stride - 1) // stride, 0)
    step_index = first_step[..., None] + jnp.arange(slot_count, dtype=jnp.int32)
    global_block = offset_vec[..., None] + stride * step_index
    local_block = global_block - base_block[..., None]
    usable = (step_index < block_count) & (local_block >= 0) & (local_block < block_count)
    return (jnp.clip(local_block, 0, block_count - 1), usable.astype(jnp.float32))


def segment_slots(shift_vec, span_len, block_count):
    device_col = jnp.arange(span_len, dtype=jnp.int32)[:, None]
    seg_block, seg_usable = slot_table(device_col, shift_vec[None, :], span_len, block_count)
    return (seg_block.transpose(1, 0, 2), seg_usable.transpose(1, 0, 2))


def select_table(local_block, block_count):
    return (local_block[..., None] == jnp.arange(block_count, dtype=jnp.int32)).astype(jnp.float32)


def pick_blocks(data, table):
    head_count, block_count = (data.shape[0], data.shape[1])
    flat = data.reshape(head_count, block_count, -1).astype(jnp.float32)
    chosen = jnp.einsum(
        "hsb,hbx->hsx",
        table,
        flat,
        precision=lax.Precision.HIGHEST,
        preferred_element_type=jnp.float32,
    ).astype(data.dtype)
    return chosen.reshape((head_count, -1) + data.shape[3:])


def place_rows(accum, contrib, table, usable):
    head_count, block_count = (accum.shape[0], accum.shape[1])
    slot_count = table.shape[1]
    weights = table * usable[..., None]
    shaped = contrib.reshape(head_count, slot_count, -1)
    added = jnp.einsum(
        "hsb,hsx->hbx",
        weights,
        shaped,
        precision=lax.Precision.HIGHEST,
        preferred_element_type=jnp.float32,
    )
    return accum + added.reshape(accum.shape)


def attend(
    query_rows,
    dout_rows,
    norm_rows,
    query_mask,
    key_rows,
    value_rows,
    key_mask,
    score_scale,
    row_block,
):
    head_count, query_count, head_dim = query_rows.shape
    steps = query_count // row_block

    def split(array):
        return jnp.moveaxis(array.reshape((head_count, steps, row_block) + array.shape[2:]), 1, 0)

    def step_fn(carry, parts):
        query_blk, dout_blk, norm_blk, mask_blk = parts
        scores = (
            jnp.einsum("hqd,hkd->hqk", query_blk, key_rows, preferred_element_type=jnp.float32)
            * score_scale
        )
        probs = jnp.exp(scores - norm_blk[:, :, None]) * mask_blk[:, :, None] * key_mask[:, None, :]
        probs_low = probs.astype(jnp.bfloat16)
        prob_grad = jnp.einsum(
            "hqd,hkd->hqk", dout_blk, value_rows, preferred_element_type=jnp.float32
        )
        dscore = (probs * prob_grad).astype(jnp.bfloat16)
        query_grad = (
            jnp.einsum("hqk,hkd->hqd", dscore, key_rows, preferred_element_type=jnp.float32)
            * score_scale
        )
        key_part = (
            jnp.einsum("hqk,hqd->hkd", dscore, query_blk, preferred_element_type=jnp.float32)
            * score_scale
        )
        value_part = jnp.einsum(
            "hqk,hqd->hkd", probs_low, dout_blk, preferred_element_type=jnp.float32
        )
        return ((carry[0] + key_part, carry[1] + value_part), query_grad)

    start = jnp.zeros((head_count, key_rows.shape[1], head_dim), jnp.float32)
    totals, query_parts = lax.scan(
        step_fn,
        (start, start),
        (split(query_rows), split(dout_rows), split(norm_rows), split(query_mask)),
    )
    query_grad = jnp.moveaxis(query_parts, 0, 1).reshape(head_count, query_count, head_dim)
    return (query_grad, totals[0], totals[1])


def swap_up(payload, my_index, bit_total):
    for bit_idx in range(bit_total):
        partner = swapped(payload, "ctx", bit_idx)
        lower_half = my_index >> bit_idx & 1 == 0
        payload = jnp.where(
            lower_half,
            jnp.concatenate([payload, partner], axis=1),
            jnp.concatenate([partner, payload], axis=1),
        )
    return payload


def swap_down(sums_kv, my_index, bit_total):
    head_count = sums_kv.shape[0]
    for bit_idx in reversed(range(bit_total)):
        halves = sums_kv.reshape(head_count, 2, -1, sums_kv.shape[-1])
        lower_half = my_index >> bit_idx & 1 == 0
        kept_half = jnp.where(lower_half, halves[:, 0], halves[:, 1])
        sent_half = jnp.where(lower_half, halves[:, 1], halves[:, 0])
        sums_kv = kept_half + swapped(sent_half.astype(jnp.bfloat16), "ctx", bit_idx).astype(
            sent_half.dtype
        )
    return sums_kv


def body(queries, keys, values, grad_out, log_norm, offsets, q_gain):
    query_raw = queries[0]
    token_count, proj_width = query_raw.shape
    head_count = log_norm.shape[1]
    head_dim = proj_width // head_count
    block_count = token_count // BLOCK
    ctx_size = lax.axis_size("ctx")
    score_scale = head_dim ** (-0.5)
    scaled = (query_raw.astype(jnp.float32) * q_gain).astype(jnp.bfloat16)

    def heads(matrix):
        return (
            matrix.reshape(token_count, head_count, head_dim)
            .transpose(1, 0, 2)
            .reshape(head_count, block_count, BLOCK, head_dim)
        )

    query_all = heads(scaled)
    key_all = heads(keys[0])
    value_all = heads(values[0])
    dout_all = heads(grad_out[0])
    norm_all = log_norm[0].reshape(head_count, block_count, BLOCK)
    query_acc = jnp.zeros((head_count, block_count, BLOCK, head_dim), jnp.float32)
    kv_acc = jnp.zeros((head_count, block_count, BLOCK, 2 * head_dim), jnp.float32)
    my_index = lax.axis_index("ctx")
    for level_idx in range(LEVELS):
        span_len = min(2**level_idx, ctx_size)
        shift_vec = offsets[:, level_idx] % span_len
        local_block, usable = slot_table(my_index % span_len, shift_vec, span_len, block_count)
        table = select_table(local_block, block_count)
        slot_count = local_block.shape[1]
        row_block = BLOCK * math.gcd(slot_count, max(1, 512 // BLOCK))
        query_own = pick_blocks(query_all, table)
        dout_own = pick_blocks(dout_all, table)
        norm_own = pick_blocks(norm_all, table)
        mask_own = jnp.repeat(usable, BLOCK, axis=1)
        payload = jnp.concatenate(
            [pick_blocks(key_all, table), pick_blocks(value_all, table)], axis=2
        )
        bit_total = span_len.bit_length() - 1
        payload = swap_up(payload, my_index, bit_total)
        seg_block, seg_usable = segment_slots(shift_vec, span_len, block_count)
        seg_mask = jnp.repeat(seg_usable.reshape(head_count, -1), BLOCK, axis=1)
        level_query, level_key, level_value = attend(
            query_own,
            dout_own,
            norm_own,
            mask_own,
            payload[..., :head_dim],
            payload[..., head_dim:],
            seg_mask,
            score_scale,
            row_block,
        )
        sums_kv = jnp.concatenate([level_key, level_value], axis=2)
        sums_kv = swap_down(sums_kv, my_index, bit_total)
        query_acc = place_rows(query_acc, level_query, table, usable)
        kv_acc = place_rows(kv_acc, sums_kv, table, usable)

    def to_rows(field_acc):
        return (
            field_acc.reshape(head_count, token_count, -1)
            .transpose(1, 0, 2)
            .reshape(token_count, -1)
        )

    dq_rows = to_rows(query_acc)
    grad_queries = (dq_rows * q_gain).astype(jnp.bfloat16)
    grad_keys = to_rows(kv_acc[..., :head_dim]).astype(jnp.bfloat16)
    grad_values = to_rows(kv_acc[..., head_dim:]).astype(jnp.bfloat16)
    gain_total = lax.psum(jnp.sum(query_raw.astype(jnp.float32) * dq_rows, axis=0), ("dp", "ctx"))
    return (grad_queries[None], grad_keys[None], grad_values[None], gain_total)


def solution(mesh):
    in_specs = (
        P("dp", "ctx", None),
        P("dp", "ctx", None),
        P("dp", "ctx", None),
        P("dp", "ctx", None),
        P("dp", None, "ctx"),
        P(),
        P(),
    )
    out_specs = (P("dp", "ctx", None), P("dp", "ctx", None), P("dp", "ctx", None), P())
    return jax.shard_map(body, mesh=mesh, in_specs=in_specs, out_specs=out_specs, check_vma=False)
```

profile of v0, /device:TPU:0, one launch (start us, length us, event | category | flops | bytes accessed | tf_op | source)
XLA Modules:
  0.0 272.5 jit_solution(3529592541120777040)
XLA Ops:
  34.6 3.2 %collective-permute-start.2 = (bf16[2,256,256]{2,1,0:T(8,128)(2,1)S(1)}, bf16[2,256,256]{2,1,0:T(8,128)(2,1)S(1)}, u32[]{:S(2)}, u32[]{:S(2)}) collective-permute-start(bf16[2,256,256]{2,1,0:T(8,128)(2,1)S(1)} %maximum_select_fusion.7), channel_id=1, source_target_pairs={{0,2},{2,0},{1,3},{3,1},{4,6},{6,4},{5,7},{7,5},{8,10},{10,8},{9,1... | collective-permute-start | bytes 786440 | tf_op jit(solution)/shard_map/ppermute | solution.py:18
  47.9 9.2 %collective-permute-done.4 = bf16[2,256,256]{2,1,0:T(8,128)(2,1)} collective-permute-done((bf16[2,256,256]{2,1,0:T(8,128)(2,1)}, bf16[2,256,256]{2,1,0:T(8,128)(2,1)}, u32[]{:S(2)}, u32[]{:S(2)}) %collective-permute-start.4) | collective-permute-done | bytes 262176 | tf_op jit(solution)/shard_map/ppermute | solution.py:18
  58.4 2.4 collective-permute-start.5
  63.1 3.0 %collective-permute-start.11 = (bf16[2,256,256]{2,1,0:T(8,128)(2,1)}, bf16[2,256,256]{2,1,0:T(8,128)(2,1)}, u32[]{:S(2)}, u32[]{:S(2)}) collective-permute-start(bf16[2,256,256]{2,1,0:T(8,128)(2,1)} %fusion.49), channel_id=1, source_target_pairs={{0,2},{2,0},{1,3},{3,1},{4,6},{6,4},{5,7},{7,5},{8,10},{10,8},{9,1... | collective-permute-start | bytes 786440 | tf_op jit(solution)/shard_map/ppermute | solution.py:18
  68.4 4.8 %collective-permute-done.5 = bf16[2,512,256]{2,1,0:T(8,128)(2,1)} collective-permute-done((bf16[2,512,256]{2,1,0:T(8,128)(2,1)S(1)}, bf16[2,512,256]{2,1,0:T(8,128)(2,1)}, u32[]{:S(2)}, u32[]{:S(2)}) %collective-permute-start.5) | collective-permute-done | bytes 524320 | tf_op jit(solution)/shard_map/ppermute | solution.py:18
  78.5 3.0 %reshape.1673 = f32[2,2,512,256]{2,1,3,0:T(2,128)S(1)} reshape(f32[2,1024,256]{1,2,0:T(8,128)} %pad_maximum_fusion.1) | data formatting | bytes 4194304 | tf_op jit(solution)/shard_map/reshape | solution.py:137
  81.6 2.9 %fusion.212 = (f32[2,1,512,256]{2,1,3,0:T(1,128)}, f32[2,1,512,256]{2,1,3,0:T(1,128)}) fusion(f32[2,2,512,256]{2,1,3,0:T(2,128)S(1)} %reshape.1673), kind=kLoop, calls=%fused_computation.413 | loop fusion | bytes 4194304 | tf_op jit(solution)/shard_map/slice | solution.py:139
  86.9 2.4 copy.152
  89.4 2.7 collective-permute-start.13
  93.8 3.7 %collective-permute-start.9 = (bf16[2,1024,256]{2,1,0:T(8,128)(2,1)S(1)}, bf16[2,1024,256]{2,1,0:T(8,128)(2,1)S(1)}, u32[]{:S(2)}, u32[]{:S(2)}) collective-permute-start(bf16[2,1024,256]{2,1,0:T(8,128)(2,1)S(1)} %maximum_select_fusion.2), channel_id=1, source_target_pairs={{0,8},{8,0},{1,9},{9,1},{2,10},{10,2},{3,11},{11,3},{4,12},{12,4},... | collective-permute-start | bytes 3145736 | tf_op jit(solution)/shard_map/ppermute | solution.py:18
  105.2 18.4 %collective-permute-done.9 = bf16[2,1024,256]{2,1,0:T(8,128)(2,1)S(1)} collective-permute-done((bf16[2,1024,256]{2,1,0:T(8,128)(2,1)S(1)}, bf16[2,1024,256]{2,1,0:T(8,128)(2,1)S(1)}, u32[]{:S(2)}, u32[]{:S(2)}) %collective-permute-start.9) | collective-permute-done | bytes 1048608 | tf_op jit(solution)/shard_map/ppermute | solution.py:18
  127.4 2.5 pad_maximum_fusion
  129.9 6.6 %reshape.1677 = f32[2,2,1024,256]{2,1,3,0:T(2,128)} reshape(f32[2,2048,256]{1,2,0:T(8,128)} %pad_maximum_fusion) | data formatting | bytes 8388608 | tf_op jit(solution)/shard_map/reshape | solution.py:137
  136.5 9.1 %fusion.211 = (f32[2,1,1024,256]{2,1,3,0:T(1,128)}, f32[2,1,1024,256]{2,1,3,0:T(1,128)}) fusion(f32[2,2,1024,256]{2,1,3,0:T(2,128)} %reshape.1677), kind=kLoop, calls=%fused_computation.412 | loop fusion | bytes 8388608 | tf_op jit(solution)/shard_map/slice | solution.py:139
  145.6 4.6 %copy.157 = f32[2,1,1024,256]{3,2,0,1:T(8,128)S(1)} copy(f32[2,1,1024,256]{2,1,3,0:T(1,128)} %get-tuple-element.141) | data formatting | bytes 4194304
  150.2 6.0 %copy.158 = f32[2,1,1024,256]{3,2,0,1:T(8,128)} copy(f32[2,1,1024,256]{2,1,3,0:T(1,128)} %get-tuple-element.142) | data formatting | bytes 4194304
  158.3 3.1 %collective-permute-start.14 = (bf16[2,256,256]{2,1,0:T(8,128)(2,1)S(1)}, bf16[2,256,256]{2,1,0:T(8,128)(2,1)S(1)}, u32[]{:S(2)}, u32[]{:S(2)}) collective-permute-start(bf16[2,256,256]{2,1,0:T(8,128)(2,1)S(1)} %fusion.50), channel_id=1, source_target_pairs={{0,2},{2,0},{1,3},{3,1},{4,6},{6,4},{5,7},{7,5},{8,10},{10,8},{9,1... | collective-permute-start | bytes 786440 | tf_op jit(solution)/shard_map/ppermute | solution.py:18
  163.7 3.3 %collective-permute-done.14 = bf16[2,256,256]{2,1,0:T(8,128)(2,1)S(1)} collective-permute-done((bf16[2,256,256]{2,1,0:T(8,128)(2,1)S(1)}, bf16[2,256,256]{2,1,0:T(8,128)(2,1)S(1)}, u32[]{:S(2)}, u32[]{:S(2)}) %collective-permute-start.14) | collective-permute-done | bytes 262176 | tf_op jit(solution)/shard_map/ppermute | solution.py:18
  167.9 14.9 %collective-permute-done.16 = bf16[2,1024,256]{2,1,0:T(8,128)(2,1)S(1)} collective-permute-done((bf16[2,1024,256]{2,1,0:T(8,128)(2,1)S(1)}, bf16[2,1024,256]{2,1,0:T(8,128)(2,1)S(1)}, u32[]{:S(2)}, u32[]{:S(2)}) %collective-permute-start.16) | collective-permute-done | bytes 1048608 | tf_op jit(solution)/shard_map/ppermute | solution.py:18
  185.6 6.9 %collective-permute-done.17 = bf16[2,512,256]{2,1,0:T(8,128)(2,1)S(1)} collective-permute-done((bf16[2,512,256]{2,1,0:T(8,128)(2,1)S(1)}, bf16[2,512,256]{2,1,0:T(8,128)(2,1)S(1)}, u32[]{:S(2)}, u32[]{:S(2)}) %collective-permute-start.17) | collective-permute-done | bytes 524320 | tf_op jit(solution)/shard_map/ppermute | solution.py:18
  193.5 3.5 %collective-permute-start.18 = (bf16[2,256,256]{2,1,0:T(8,128)(2,1)}, bf16[2,256,256]{2,1,0:T(8,128)(2,1)S(1)}, u32[]{:S(2)}, u32[]{:S(2)}) collective-permute-start(bf16[2,256,256]{2,1,0:T(8,128)(2,1)} %fusion.51), channel_id=1, source_target_pairs={{0,2},{2,0},{1,3},{3,1},{4,6},{6,4},{5,7},{7,5},{8,10},{10,8},{9,1... | collective-permute-start | bytes 786440 | tf_op jit(solution)/shard_map/ppermute | solution.py:18
  199.1 63.0 %psum.7 = f32[256]{0:T(256)} all-reduce(f32[256]{0:T(256)S(1)} %bitcast.569), channel_id=1, replica_groups=mesh['dp'=8,'ctx'=16] {'dp','ctx'}, use_global_device_ids=true, to_apply=%region_1.2 | all-reduce | flops 256 | bytes 2048 | tf_op jit(solution)/shard_map/psum | solution.py:217
  264.4 3.2 %collective-permute-done.19 = bf16[2,128,256]{2,1,0:T(8,128)(2,1)S(1)} collective-permute-done((bf16[2,128,256]{2,1,0:T(8,128)(2,1)S(1)}, bf16[2,128,256]{2,1,0:T(8,128)(2,1)S(1)}, u32[]{:S(2)}, u32[]{:S(2)}) %collective-permute-start.19) | collective-permute-done | bytes 131104 | tf_op jit(solution)/shard_map/ppermute | solution.py:18
  267.9 2.4 fusion.3
  (336 shorter events, 85.3 us)
Async XLA Ops:
  5.4 26.5 %collective-permute-start = (bf16[2,128,256]{2,1,0:T(8,128)(2,1)S(1)}, bf16[2,128,256]{2,1,0:T(8,128)(2,1)S(1)}, u32[]{:S(2)}, u32[]{:S(2)}) collective-permute-start(bf16[2,128,256]{2,1,0:T(8,128)(2,1)S(1)} %bitcast_dynamic-update-slice_fusion.6), channel_id=1, source_target_pairs={{0,1},{1,0},{2,3},{3,2},{4,5},{5,4},{6,7},{7,6},{8,9},{9,8},{10,11... | collective-permute-start | bytes 393224 | tf_op jit(solution)/shard_map/ppermute | solution.py:18
  7.9 26.5 %collective-permute-start.1 = (bf16[2,128,256]{2,1,0:T(8,128)(2,1)S(1)}, bf16[2,128,256]{2,1,0:T(8,128)(2,1)S(1)}, u32[]{:S(2)}, u32[]{:S(2)}) collective-permute-start(bf16[2,128,256]{2,1,0:T(8,128)(2,1)S(1)} %bitcast_dynamic-update-slice_fusion.4), channel_id=1, source_target_pairs={{0,1},{1,0},{2,3},{3,2},{4,5},{5,4},{6,7},{7,6},{8,9},{9,8},{10,11... | collective-permute-start | bytes 393224 | tf_op jit(solution)/shard_map/ppermute | solution.py:18
  9.4 32.7 %collective-permute-start.3 = (bf16[2,128,256]{2,1,0:T(8,128)(2,1)S(1)}, bf16[2,128,256]{2,1,0:T(8,128)(2,1)S(1)}, u32[]{:S(2)}, u32[]{:S(2)}) collective-permute-start(bf16[2,128,256]{2,1,0:T(8,128)(2,1)S(1)} %bitcast_dynamic-update-slice_fusion.2), channel_id=1, source_target_pairs={{0,1},{1,0},{2,3},{3,2},{4,5},{5,4},{6,7},{7,6},{8,9},{9,8},{10,11... | collective-permute-start | bytes 393224 | tf_op jit(solution)/shard_map/ppermute | solution.py:18
  11.9 27.4 %collective-permute-start.6 = (bf16[2,128,256]{2,1,0:T(8,128)(2,1)S(1)}, bf16[2,128,256]{2,1,0:T(8,128)(2,1)S(1)}, u32[]{:S(2)}, u32[]{:S(2)}) collective-permute-start(bf16[2,128,256]{2,1,0:T(8,128)(2,1)S(1)} %bitcast_dynamic-update-slice_fusion), channel_id=1, source_target_pairs={{0,1},{1,0},{2,3},{3,2},{4,5},{5,4},{6,7},{7,6},{8,9},{9,8},{10,11... | collective-permute-start | bytes 393224 | tf_op jit(solution)/shard_map/ppermute | solution.py:18
  34.6 10.8 %collective-permute-start.2 = (bf16[2,256,256]{2,1,0:T(8,128)(2,1)S(1)}, bf16[2,256,256]{2,1,0:T(8,128)(2,1)S(1)}, u32[]{:S(2)}, u32[]{:S(2)}) collective-permute-start(bf16[2,256,256]{2,1,0:T(8,128)(2,1)S(1)} %maximum_select_fusion.7), channel_id=1, source_target_pairs={{0,2},{2,0},{1,3},{3,1},{4,6},{6,4},{5,7},{7,5},{8,10},{10,8},{9,1... | collective-permute-start | bytes 786440 | tf_op jit(solution)/shard_map/ppermute | solution.py:18
  38.7 58.8 %collective-permute-start.10 = (bf16[2,128,256]{2,1,0:T(8,128)(2,1)}, bf16[2,128,256]{2,1,0:T(8,128)(2,1)}, u32[]{:S(2)}, u32[]{:S(2)}) collective-permute-start(bf16[2,128,256]{2,1,0:T(8,128)(2,1)} %fusion.67), channel_id=1, source_target_pairs={{0,1},{1,0},{2,3},{3,2},{4,5},{5,4},{6,7},{7,6},{8,9},{9,8},{10,11... | collective-permute-start | bytes 393224 | tf_op jit(solution)/shard_map/ppermute | solution.py:18
  40.1 26.1 %collective-permute-start.7 = (bf16[2,256,256]{2,1,0:T(8,128)(2,1)}, bf16[2,256,256]{2,1,0:T(8,128)(2,1)}, u32[]{:S(2)}, u32[]{:S(2)}) collective-permute-start(bf16[2,256,256]{2,1,0:T(8,128)(2,1)} %maximum_select_fusion.9), channel_id=1, source_target_pairs={{0,2},{2,0},{1,3},{3,1},{4,6},{6,4},{5,7},{7,5},{8,10},{10,8},{9,1... | collective-permute-start | bytes 786440 | tf_op jit(solution)/shard_map/ppermute | solution.py:18
  42.9 14.2 %collective-permute-start.4 = (bf16[2,256,256]{2,1,0:T(8,128)(2,1)}, bf16[2,256,256]{2,1,0:T(8,128)(2,1)}, u32[]{:S(2)}, u32[]{:S(2)}) collective-permute-start(bf16[2,256,256]{2,1,0:T(8,128)(2,1)} %maximum_select_fusion.8), channel_id=1, source_target_pairs={{0,2},{2,0},{1,3},{3,1},{4,6},{6,4},{5,7},{7,5},{8,10},{10,8},{9,1... | collective-permute-start | bytes 786440 | tf_op jit(solution)/shard_map/ppermute | solution.py:18
  58.4 14.8 %collective-permute-start.5 = (bf16[2,512,256]{2,1,0:T(8,128)(2,1)S(1)}, bf16[2,512,256]{2,1,0:T(8,128)(2,1)}, u32[]{:S(2)}, u32[]{:S(2)}) collective-permute-start(bf16[2,512,256]{2,1,0:T(8,128)(2,1)S(1)} %maximum_select_fusion.4), channel_id=1, source_target_pairs={{0,4},{4,0},{1,5},{5,1},{2,6},{6,2},{3,7},{7,3},{8,12},{12,8},{9,1... | collective-permute-start | bytes 1572872 | tf_op jit(solution)/shard_map/ppermute | solution.py:18
  63.1 36.2 %collective-permute-start.11 = (bf16[2,256,256]{2,1,0:T(8,128)(2,1)}, bf16[2,256,256]{2,1,0:T(8,128)(2,1)}, u32[]{:S(2)}, u32[]{:S(2)}) collective-permute-start(bf16[2,256,256]{2,1,0:T(8,128)(2,1)} %fusion.49), channel_id=1, source_target_pairs={{0,2},{2,0},{1,3},{3,1},{4,6},{6,4},{5,7},{7,5},{8,10},{10,8},{9,1... | collective-permute-start | bytes 786440 | tf_op jit(solution)/shard_map/ppermute | solution.py:18
  68.3 23.8 %collective-permute-start.8 = (bf16[2,512,256]{2,1,0:T(8,128)(2,1)}, bf16[2,512,256]{2,1,0:T(8,128)(2,1)}, u32[]{:S(2)}, u32[]{:S(2)}) collective-permute-start(bf16[2,512,256]{2,1,0:T(8,128)(2,1)} %maximum_select_fusion.5), channel_id=1, source_target_pairs={{0,4},{4,0},{1,5},{5,1},{2,6},{6,2},{3,7},{7,3},{8,12},{12,8},{9,1... | collective-permute-start | bytes 1572872 | tf_op jit(solution)/shard_map/ppermute | solution.py:18
  89.4 15.5 %collective-permute-start.13 = (bf16[2,512,256]{2,1,0:T(8,128)(2,1)S(1)}, bf16[2,512,256]{2,1,0:T(8,128)(2,1)S(1)}, u32[]{:S(2)}, u32[]{:S(2)}) collective-permute-start(bf16[2,512,256]{2,1,0:T(8,128)(2,1)S(1)} %fusion.42), channel_id=1, source_target_pairs={{0,4},{4,0},{1,5},{5,1},{2,6},{6,2},{3,7},{7,3},{8,12},{12,8},{9,1... | collective-permute-start | bytes 1572872 | tf_op jit(solution)/shard_map/ppermute | solution.py:18
  93.8 29.7 %collective-permute-start.9 = (bf16[2,1024,256]{2,1,0:T(8,128)(2,1)S(1)}, bf16[2,1024,256]{2,1,0:T(8,128)(2,1)S(1)}, u32[]{:S(2)}, u32[]{:S(2)}) collective-permute-start(bf16[2,1024,256]{2,1,0:T(8,128)(2,1)S(1)} %maximum_select_fusion.2), channel_id=1, source_target_pairs={{0,8},{8,0},{1,9},{9,1},{2,10},{10,2},{3,11},{11,3},{4,12},{12,4},... | collective-permute-start | bytes 3145736 | tf_op jit(solution)/shard_map/ppermute | solution.py:18
  101.1 60.6 %collective-permute-start.12 = (bf16[2,128,256]{2,1,0:T(8,128)(2,1)}, bf16[2,128,256]{2,1,0:T(8,128)(2,1)}, u32[]{:S(2)}, u32[]{:S(2)}) collective-permute-start(bf16[2,128,256]{2,1,0:T(8,128)(2,1)} %fusion.68), channel_id=1, source_target_pairs={{0,1},{1,0},{2,3},{3,2},{4,5},{5,4},{6,7},{7,6},{8,9},{9,8},{10,11... | collective-permute-start | bytes 393224 | tf_op jit(solution)/shard_map/ppermute | solution.py:18
  158.1 24.7 %collective-permute-start.16 = (bf16[2,1024,256]{2,1,0:T(8,128)(2,1)S(1)}, bf16[2,1024,256]{2,1,0:T(8,128)(2,1)S(1)}, u32[]{:S(2)}, u32[]{:S(2)}) collective-permute-start(bf16[2,1024,256]{2,1,0:T(8,128)(2,1)S(1)} %fusion.36), channel_id=1, source_target_pairs={{0,8},{8,0},{1,9},{9,1},{2,10},{10,2},{3,11},{11,3},{4,12},{12,4},... | collective-permute-start | bytes 3145736 | tf_op jit(solution)/shard_map/ppermute | solution.py:18
  158.3 8.7 %collective-permute-start.14 = (bf16[2,256,256]{2,1,0:T(8,128)(2,1)S(1)}, bf16[2,256,256]{2,1,0:T(8,128)(2,1)S(1)}, u32[]{:S(2)}, u32[]{:S(2)}) collective-permute-start(bf16[2,256,256]{2,1,0:T(8,128)(2,1)S(1)} %fusion.50), channel_id=1, source_target_pairs={{0,2},{2,0},{1,3},{3,1},{4,6},{6,4},{5,7},{7,5},{8,10},{10,8},{9,1... | collective-permute-start | bytes 786440 | tf_op jit(solution)/shard_map/ppermute | solution.py:18
  167.1 16.7 %collective-permute-start.15 = (bf16[2,128,256]{2,1,0:T(8,128)(2,1)S(1)}, bf16[2,128,256]{2,1,0:T(8,128)(2,1)S(1)}, u32[]{:S(2)}, u32[]{:S(2)}) collective-permute-start(bf16[2,128,256]{2,1,0:T(8,128)(2,1)S(1)} %fusion.69), channel_id=1, source_target_pairs={{0,1},{1,0},{2,3},{3,2},{4,5},{5,4},{6,7},{7,6},{8,9},{9,8},{10,11... | collective-permute-start | bytes 393224 | tf_op jit(solution)/shard_map/ppermute | solution.py:18
  183.3 9.3 %collective-permute-start.17 = (bf16[2,512,256]{2,1,0:T(8,128)(2,1)S(1)}, bf16[2,512,256]{2,1,0:T(8,128)(2,1)S(1)}, u32[]{:S(2)}, u32[]{:S(2)}) collective-permute-start(bf16[2,512,256]{2,1,0:T(8,128)(2,1)S(1)} %fusion.43), channel_id=1, source_target_pairs={{0,4},{4,0},{1,5},{5,1},{2,6},{6,2},{3,7},{7,3},{8,12},{12,8},{9,1... | collective-permute-start | bytes 1572872 | tf_op jit(solution)/shard_map/ppermute | solution.py:18
  193.5 68.7 %collective-permute-start.18 = (bf16[2,256,256]{2,1,0:T(8,128)(2,1)}, bf16[2,256,256]{2,1,0:T(8,128)(2,1)S(1)}, u32[]{:S(2)}, u32[]{:S(2)}) collective-permute-start(bf16[2,256,256]{2,1,0:T(8,128)(2,1)} %fusion.51), channel_id=1, source_target_pairs={{0,2},{2,0},{1,3},{3,1},{4,6},{6,4},{5,7},{7,5},{8,10},{10,8},{9,1... | collective-permute-start | bytes 786440 | tf_op jit(solution)/shard_map/ppermute | solution.py:18
  198.3 65.4 %copy-start.37 = (f32[256]{0:T(256)S(1)}, f32[256]{0:T(256)}, u32[]{:S(2)}) copy-start(f32[256]{0:T(256)} %param.13) | copy-start | bytes 3076
  199.1 68.8 %copy-start.17 = (f32[2,2,32768]{2,1,0:T(2,128)S(1)}, f32[2,2,32768]{2,1,0:T(2,128)}, u32[]{:S(2)}) copy-start(f32[2,2,32768]{2,1,0:T(2,128)} %reshape.1667) | copy-start | bytes 1572868
  199.1 68.8 %copy-start.21 = (f32[1,2,128,256]{3,1,2,0:T(2,128)S(1)}, f32[1,2,128,256]{3,1,2,0:T(2,128)}, u32[]{:S(2)}) copy-start(f32[1,2,128,256]{3,1,2,0:T(2,128)} %copy.191) | copy-start | bytes 786436
  199.1 68.8 %copy-start.22 = (f32[1,2,128,256]{3,1,2,0:T(2,128)S(1)}, f32[1,2,128,256]{3,1,2,0:T(2,128)}, u32[]{:S(2)}) copy-start(f32[1,2,128,256]{3,1,2,0:T(2,128)} %copy.192) | copy-start | bytes 786436
  262.3 5.3 %collective-permute-start.19 = (bf16[2,128,256]{2,1,0:T(8,128)(2,1)S(1)}, bf16[2,128,256]{2,1,0:T(8,128)(2,1)S(1)}, u32[]{:S(2)}, u32[]{:S(2)}) collective-permute-start(bf16[2,128,256]{2,1,0:T(8,128)(2,1)S(1)} %fusion.70), channel_id=1, source_target_pairs={{0,1},{1,0},{2,3},{3,2},{4,5},{5,4},{6,7},{7,6},{8,9},{9,8},{10,11... | collective-permute-start | bytes 393224 | tf_op jit(solution)/shard_map/ppermute | solution.py:18
  (59 other events, 445.6 us)
where the time goes:
time: 277 us; the launch traced here: 273 us
  waiting for transfers between devices  63.6 us (23%)
  blocking collectives  63 us (23%)
  local copies, waits for them, and re-layouts  59.3 us (21%)
  starting transfers between devices  34.9 us (13%)
  other arithmetic  27.5 us (10%)
  matrix products  21.6 us (8%)
    ppermute x20, waiting for transfers between devices, swapped(): return lax.ppermute(block, axis, route)  63.6 us
    psum x1, blocking collectives, body(): lax.psum(jnp.sum(query_raw.astype(jnp.float32) * dq_rows, axis=0), ('dp',...  63 us
    ppermute x20, starting transfers between devices, swapped(): return lax.ppermute(block, axis, route)  34.9 us
    unnamed x153, local copies, waits for them, and re-layouts  24.8 us
    slice x3, local copies, waits for them, and re-layouts, swap_down(): kept_half = jnp.where(lower_half, halves[:, 0], halves[:, 1])  12.9 us
    reshape x3, local copies, waits for them, and re-layouts, swap_down(): halves = sums_kv.reshape(head_count, 2, -1, sums_kv.shape[-1])  10.3 us
    dot_general x25, matrix products, pick_blocks(): jnp.einsum('hsb,hbx->hsx', table, flat, precision=lax.Precision.HIGHEST,...  10.3 us
    select_n x10, other arithmetic, swap_up(): jnp.where(lower_half, jnp.concatenate([payload, partner], axis=1), jnp.co...  9.27 us
  transfers between devices with their start and end apart: 20, of which 9 were waited for; matrix products, arithmetic and copies ran while one was open for 34% of the time, Pallas kernels for 0%

commit v1 on v0

--- a/solution.py
+++ b/solution.py
@@ -214,7 +214,9 @@
     grad_queries = (dq_rows * q_gain).astype(jnp.bfloat16)
     grad_keys = to_rows(kv_acc[..., :head_dim]).astype(jnp.bfloat16)
     grad_values = to_rows(kv_acc[..., head_dim:]).astype(jnp.bfloat16)
-    gain_total = lax.psum(jnp.sum(query_raw.astype(jnp.float32) * dq_rows, axis=0), ("dp", "ctx"))
+    part = jnp.sum(query_raw.astype(jnp.float32) * dq_rows, axis=0)
+    pieces = lax.all_gather(part, ("dp", "ctx"), axis=0, tiled=False)
+    gain_total = pieces.sum(axis=0)
     return (grad_queries[None], grad_keys[None], grad_values[None], gain_total)
 
 

time: 277 us -> 265 us (0.957)
  the two profiles are of different devices: /device:TPU:0 before, /device:TPU:1 now
where the time goes in v1:
time: 265 us; the launch traced here: 260 us
  blocking collectives  61.7 us (23%)
  local copies, waits for them, and re-layouts  59.1 us (22%)
  waiting for transfers between devices  56.8 us (21%)
  starting transfers between devices  29.3 us (11%)
  other arithmetic  29.2 us (11%)
  matrix products  21.7 us (8%)
    all_gather x1, blocking collectives, body(): pieces = lax.all_gather(part, ('dp', 'ctx'), axis=0, tiled=False)  61.7 us
    ppermute x20, waiting for transfers between devices, swapped(): return lax.ppermute(block, axis, route)  56.8 us
    ppermute x20, starting transfers between devices, swapped(): return lax.ppermute(block, axis, route)  29.3 us
    unnamed x153, local copies, waits for them, and re-layouts  24.6 us
    slice x3, local copies, waits for them, and re-layouts, swap_down(): kept_half = jnp.where(lower_half, halves[:, 0], halves[:, 1])  12.9 us
    reshape x3, local copies, waits for them, and re-layouts, swap_down(): halves = sums_kv.reshape(head_count, 2, -1, sums_kv.shape[-1])  10.3 us
    dot_general x25, matrix products, pick_blocks(): jnp.einsum('hsb,hbx->hsx', table, flat, precision=lax.Precision.HIGHEST,...  10.3 us
    select_n x10, other arithmetic, swap_up(): jnp.where(lower_half, jnp.concatenate([payload, partner], axis=1), jnp.co...  9.28 us
  transfers between devices with their start and end apart: 20, of which 7 were waited for; matrix products, arithmetic and copies ran while one was open for 36% of the time, Pallas kernels for 0%

profile of v1, /device:TPU:1, one launch (start us, length us, event | category | flops | bytes accessed | tf_op | source)
XLA Modules:
  0.0 260.3 jit_solution(7653714906080200234)
XLA Ops:
  34.1 3.0 %collective-permute-start.2 = (bf16[2,256,256]{2,1,0:T(8,128)(2,1)S(1)}, bf16[2,256,256]{2,1,0:T(8,128)(2,1)S(1)}, u32[]{:S(2)}, u32[]{:S(2)}) collective-permute-start(bf16[2,256,256]{2,1,0:T(8,128)(2,1)S(1)} %maximum_select_fusion.7), channel_id=1, source_target_pairs={{0,2},{2,0},{1,3},{3,1},{4,6},{6,4},{5,7},{7,5},{8,10},{10,8},{9,1... | collective-permute-start | bytes 786440 | tf_op jit(solution)/shard_map/ppermute | solution.py:18
  45.5 10.2 %collective-permute-done.4 = bf16[2,256,256]{2,1,0:T(8,128)(2,1)} collective-permute-done((bf16[2,256,256]{2,1,0:T(8,128)(2,1)}, bf16[2,256,256]{2,1,0:T(8,128)(2,1)}, u32[]{:S(2)}, u32[]{:S(2)}) %collective-permute-start.4) | collective-permute-done | bytes 262176 | tf_op jit(solution)/shard_map/ppermute | solution.py:18
  57.0 2.2 collective-permute-start.5
  61.5 2.7 %collective-permute-start.11 = (bf16[2,256,256]{2,1,0:T(8,128)(2,1)}, bf16[2,256,256]{2,1,0:T(8,128)(2,1)}, u32[]{:S(2)}, u32[]{:S(2)}) collective-permute-start(bf16[2,256,256]{2,1,0:T(8,128)(2,1)} %fusion.49), channel_id=1, source_target_pairs={{0,2},{2,0},{1,3},{3,1},{4,6},{6,4},{5,7},{7,5},{8,10},{10,8},{9,1... | collective-permute-start | bytes 786440 | tf_op jit(solution)/shard_map/ppermute | solution.py:18
  64.3 2.2 maximum_select_fusion.5
  66.5 2.4 collective-permute-done.5
  74.2 3.0 %reshape.1674 = f32[2,2,512,256]{2,1,3,0:T(2,128)S(1)} reshape(f32[2,1024,256]{1,2,0:T(8,128)} %pad_maximum_fusion.1) | data formatting | bytes 4194304 | tf_op jit(solution)/shard_map/reshape | solution.py:137
  77.2 2.9 %fusion.212 = (f32[2,1,512,256]{2,1,3,0:T(1,128)}, f32[2,1,512,256]{2,1,3,0:T(1,128)}) fusion(f32[2,2,512,256]{2,1,3,0:T(2,128)S(1)} %reshape.1674), kind=kLoop, calls=%fused_computation.413 | loop fusion | bytes 4194304 | tf_op jit(solution)/shard_map/slice | solution.py:139
  80.2 2.3 copy.200
  82.5 2.4 copy.201
  88.1 3.4 %collective-permute-start.9 = (bf16[2,1024,256]{2,1,0:T(8,128)(2,1)S(1)}, bf16[2,1024,256]{2,1,0:T(8,128)(2,1)S(1)}, u32[]{:S(2)}, u32[]{:S(2)}) collective-permute-start(bf16[2,1024,256]{2,1,0:T(8,128)(2,1)S(1)} %maximum_select_fusion.2), channel_id=1, source_target_pairs={{0,8},{8,0},{1,9},{9,1},{2,10},{10,2},{3,11},{11,3},{4,12},{12,4},... | collective-permute-start | bytes 3145736 | tf_op jit(solution)/shard_map/ppermute | solution.py:18
  96.8 20.4 %collective-permute-done.9 = bf16[2,1024,256]{2,1,0:T(8,128)(2,1)S(1)} collective-permute-done((bf16[2,1024,256]{2,1,0:T(8,128)(2,1)S(1)}, bf16[2,1024,256]{2,1,0:T(8,128)(2,1)S(1)}, u32[]{:S(2)}, u32[]{:S(2)}) %collective-permute-start.9) | collective-permute-done | bytes 1048608 | tf_op jit(solution)/shard_map/ppermute | solution.py:18
  121.1 2.5 pad_maximum_fusion
  123.6 6.6 %reshape.1678 = f32[2,2,1024,256]{2,1,3,0:T(2,128)} reshape(f32[2,2048,256]{1,2,0:T(8,128)} %pad_maximum_fusion) | data formatting | bytes 8388608 | tf_op jit(solution)/shard_map/reshape | solution.py:137
  130.2 9.1 %fusion.211 = (f32[2,1,1024,256]{2,1,3,0:T(1,128)}, f32[2,1,1024,256]{2,1,3,0:T(1,128)}) fusion(f32[2,2,1024,256]{2,1,3,0:T(2,128)} %reshape.1678), kind=kLoop, calls=%fused_computation.412 | loop fusion | bytes 8388608 | tf_op jit(solution)/shard_map/slice | solution.py:139
  139.3 4.6 %copy.206 = f32[2,1,1024,256]{3,2,0,1:T(8,128)S(1)} copy(f32[2,1,1024,256]{2,1,3,0:T(1,128)} %get-tuple-element.141) | data formatting | bytes 4194304
  143.8 6.0 %copy.207 = f32[2,1,1024,256]{3,2,0,1:T(8,128)} copy(f32[2,1,1024,256]{2,1,3,0:T(1,128)} %get-tuple-element.142) | data formatting | bytes 4194304
  151.9 2.8 %collective-permute-start.14 = (bf16[2,256,256]{2,1,0:T(8,128)(2,1)S(1)}, bf16[2,256,256]{2,1,0:T(8,128)(2,1)S(1)}, u32[]{:S(2)}, u32[]{:S(2)}) collective-permute-start(bf16[2,256,256]{2,1,0:T(8,128)(2,1)S(1)} %fusion.50), channel_id=1, source_target_pairs={{0,2},{2,0},{1,3},{3,1},{4,6},{6,4},{5,7},{7,5},{8,10},{10,8},{9,1... | collective-permute-start | bytes 786440 | tf_op jit(solution)/shard_map/ppermute | solution.py:18
  160.1 10.1 %collective-permute-done.16 = bf16[2,1024,256]{2,1,0:T(8,128)(2,1)S(1)} collective-permute-done((bf16[2,1024,256]{2,1,0:T(8,128)(2,1)S(1)}, bf16[2,1024,256]{2,1,0:T(8,128)(2,1)S(1)}, u32[]{:S(2)}, u32[]{:S(2)}) %collective-permute-start.16) | collective-permute-done | bytes 1048608 | tf_op jit(solution)/shard_map/ppermute | solution.py:18
  173.1 8.0 %collective-permute-done.17 = bf16[2,512,256]{2,1,0:T(8,128)(2,1)S(1)} collective-permute-done((bf16[2,512,256]{2,1,0:T(8,128)(2,1)S(1)}, bf16[2,512,256]{2,1,0:T(8,128)(2,1)S(1)}, u32[]{:S(2)}, u32[]{:S(2)}) %collective-permute-start.17) | collective-permute-done | bytes 524320 | tf_op jit(solution)/shard_map/ppermute | solution.py:18
  182.0 2.6 collective-permute-start.18
  186.6 61.7 %all-gather = f32[128,1,256]{2,1,0:T(1,128)S(1)} all-gather(f32[1,1,256]{2,1,0:T(1,128)S(1)} %bitcast.569), channel_id=1, replica_groups=mesh['dp'=8,'ctx'=16] {'dp','ctx'}, dimensions={0}, use_global_device_ids=true | all-gather | bytes 132096 | tf_op jit(solution)/shard_map/all_gather | solution.py:218
  251.4 3.9 %collective-permute-done.19 = bf16[2,128,256]{2,1,0:T(8,128)(2,1)S(1)} collective-permute-done((bf16[2,128,256]{2,1,0:T(8,128)(2,1)S(1)}, bf16[2,128,256]{2,1,0:T(8,128)(2,1)S(1)}, u32[]{:S(2)}, u32[]{:S(2)}) %collective-permute-start.19) | collective-permute-done | bytes 131104 | tf_op jit(solution)/shard_map/ppermute | solution.py:18
  255.6 2.4 fusion.3
  (337 shorter events, 80.2 us)
Async XLA Ops:
  5.4 26.0 %collective-permute-start = (bf16[2,128,256]{2,1,0:T(8,128)(2,1)S(1)}, bf16[2,128,256]{2,1,0:T(8,128)(2,1)S(1)}, u32[]{:S(2)}, u32[]{:S(2)}) collective-permute-start(bf16[2,128,256]{2,1,0:T(8,128)(2,1)S(1)} %bitcast_dynamic-update-slice_fusion.6), channel_id=1, source_target_pairs={{0,1},{1,0},{2,3},{3,2},{4,5},{5,4},{6,7},{7,6},{8,9},{9,8},{10,11... | collective-permute-start | bytes 393224 | tf_op jit(solution)/shard_map/ppermute | solution.py:18
  8.4 25.6 %collective-permute-start.1 = (bf16[2,128,256]{2,1,0:T(8,128)(2,1)S(1)}, bf16[2,128,256]{2,1,0:T(8,128)(2,1)S(1)}, u32[]{:S(2)}, u32[]{:S(2)}) collective-permute-start(bf16[2,128,256]{2,1,0:T(8,128)(2,1)S(1)} %bitcast_dynamic-update-slice_fusion.4), channel_id=1, source_target_pairs={{0,1},{1,0},{2,3},{3,2},{4,5},{5,4},{6,7},{7,6},{8,9},{9,8},{10,11... | collective-permute-start | bytes 393224 | tf_op jit(solution)/shard_map/ppermute | solution.py:18
  9.4 31.4 %collective-permute-start.3 = (bf16[2,128,256]{2,1,0:T(8,128)(2,1)S(1)}, bf16[2,128,256]{2,1,0:T(8,128)(2,1)S(1)}, u32[]{:S(2)}, u32[]{:S(2)}) collective-permute-start(bf16[2,128,256]{2,1,0:T(8,128)(2,1)S(1)} %bitcast_dynamic-update-slice_fusion.2), channel_id=1, source_target_pairs={{0,1},{1,0},{2,3},{3,2},{4,5},{5,4},{6,7},{7,6},{8,9},{9,8},{10,11... | collective-permute-start | bytes 393224 | tf_op jit(solution)/shard_map/ppermute | solution.py:18
  11.8 26.5 %collective-permute-start.6 = (bf16[2,128,256]{2,1,0:T(8,128)(2,1)S(1)}, bf16[2,128,256]{2,1,0:T(8,128)(2,1)S(1)}, u32[]{:S(2)}, u32[]{:S(2)}) collective-permute-start(bf16[2,128,256]{2,1,0:T(8,128)(2,1)S(1)} %bitcast_dynamic-update-slice_fusion), channel_id=1, source_target_pairs={{0,1},{1,0},{2,3},{3,2},{4,5},{5,4},{6,7},{7,6},{8,9},{9,8},{10,11... | collective-permute-start | bytes 393224 | tf_op jit(solution)/shard_map/ppermute | solution.py:18
  34.1 8.9 %collective-permute-start.2 = (bf16[2,256,256]{2,1,0:T(8,128)(2,1)S(1)}, bf16[2,256,256]{2,1,0:T(8,128)(2,1)S(1)}, u32[]{:S(2)}, u32[]{:S(2)}) collective-permute-start(bf16[2,256,256]{2,1,0:T(8,128)(2,1)S(1)} %maximum_select_fusion.7), channel_id=1, source_target_pairs={{0,2},{2,0},{1,3},{3,1},{4,6},{6,4},{5,7},{7,5},{8,10},{10,8},{9,1... | collective-permute-start | bytes 786440 | tf_op jit(solution)/shard_map/ppermute | solution.py:18
  38.0 53.5 %collective-permute-start.10 = (bf16[2,128,256]{2,1,0:T(8,128)(2,1)}, bf16[2,128,256]{2,1,0:T(8,128)(2,1)}, u32[]{:S(2)}, u32[]{:S(2)}) collective-permute-start(bf16[2,128,256]{2,1,0:T(8,128)(2,1)} %fusion.67), channel_id=1, source_target_pairs={{0,1},{1,0},{2,3},{3,2},{4,5},{5,4},{6,7},{7,6},{8,9},{9,8},{10,11... | collective-permute-start | bytes 393224 | tf_op jit(solution)/shard_map/ppermute | solution.py:18
  39.1 25.1 %collective-permute-start.7 = (bf16[2,256,256]{2,1,0:T(8,128)(2,1)}, bf16[2,256,256]{2,1,0:T(8,128)(2,1)}, u32[]{:S(2)}, u32[]{:S(2)}) collective-permute-start(bf16[2,256,256]{2,1,0:T(8,128)(2,1)} %maximum_select_fusion.9), channel_id=1, source_target_pairs={{0,2},{2,0},{1,3},{3,1},{4,6},{6,4},{5,7},{7,5},{8,10},{10,8},{9,1... | collective-permute-start | bytes 786440 | tf_op jit(solution)/shard_map/ppermute | solution.py:18
  41.7 13.9 %collective-permute-start.4 = (bf16[2,256,256]{2,1,0:T(8,128)(2,1)}, bf16[2,256,256]{2,1,0:T(8,128)(2,1)}, u32[]{:S(2)}, u32[]{:S(2)}) collective-permute-start(bf16[2,256,256]{2,1,0:T(8,128)(2,1)} %maximum_select_fusion.8), channel_id=1, source_target_pairs={{0,2},{2,0},{1,3},{3,1},{4,6},{6,4},{5,7},{7,5},{8,10},{10,8},{9,1... | collective-permute-start | bytes 786440 | tf_op jit(solution)/shard_map/ppermute | solution.py:18
  57.0 11.9 %collective-permute-start.5 = (bf16[2,512,256]{2,1,0:T(8,128)(2,1)S(1)}, bf16[2,512,256]{2,1,0:T(8,128)(2,1)}, u32[]{:S(2)}, u32[]{:S(2)}) collective-permute-start(bf16[2,512,256]{2,1,0:T(8,128)(2,1)S(1)} %maximum_select_fusion.4), channel_id=1, source_target_pairs={{0,4},{4,0},{1,5},{5,1},{2,6},{6,2},{3,7},{7,3},{8,12},{12,8},{9,1... | collective-permute-start | bytes 1572872 | tf_op jit(solution)/shard_map/ppermute | solution.py:18
  61.5 31.8 %collective-permute-start.11 = (bf16[2,256,256]{2,1,0:T(8,128)(2,1)}, bf16[2,256,256]{2,1,0:T(8,128)(2,1)}, u32[]{:S(2)}, u32[]{:S(2)}) collective-permute-start(bf16[2,256,256]{2,1,0:T(8,128)(2,1)} %fusion.49), channel_id=1, source_target_pairs={{0,2},{2,0},{1,3},{3,1},{4,6},{6,4},{5,7},{7,5},{8,10},{10,8},{9,1... | collective-permute-start | bytes 786440 | tf_op jit(solution)/shard_map/ppermute | solution.py:18
  66.4 19.9 %collective-permute-start.8 = (bf16[2,512,256]{2,1,0:T(8,128)(2,1)}, bf16[2,512,256]{2,1,0:T(8,128)(2,1)}, u32[]{:S(2)}, u32[]{:S(2)}) collective-permute-start(bf16[2,512,256]{2,1,0:T(8,128)(2,1)} %maximum_select_fusion.5), channel_id=1, source_target_pairs={{0,4},{4,0},{1,5},{5,1},{2,6},{6,2},{3,7},{7,3},{8,12},{12,8},{9,1... | collective-permute-start | bytes 1572872 | tf_op jit(solution)/shard_map/ppermute | solution.py:18
  85.1 11.5 %collective-permute-start.13 = (bf16[2,512,256]{2,1,0:T(8,128)(2,1)S(1)}, bf16[2,512,256]{2,1,0:T(8,128)(2,1)S(1)}, u32[]{:S(2)}, u32[]{:S(2)}) collective-permute-start(bf16[2,512,256]{2,1,0:T(8,128)(2,1)S(1)} %fusion.42), channel_id=1, source_target_pairs={{0,4},{4,0},{1,5},{5,1},{2,6},{6,2},{3,7},{7,3},{8,12},{12,8},{9,1... | collective-permute-start | bytes 1572872 | tf_op jit(solution)/shard_map/ppermute | solution.py:18
  88.1 29.1 %collective-permute-start.9 = (bf16[2,1024,256]{2,1,0:T(8,128)(2,1)S(1)}, bf16[2,1024,256]{2,1,0:T(8,128)(2,1)S(1)}, u32[]{:S(2)}, u32[]{:S(2)}) collective-permute-start(bf16[2,1024,256]{2,1,0:T(8,128)(2,1)S(1)} %maximum_select_fusion.2), channel_id=1, source_target_pairs={{0,8},{8,0},{1,9},{9,1},{2,10},{10,2},{3,11},{11,3},{4,12},{12,4},... | collective-permute-start | bytes 3145736 | tf_op jit(solution)/shard_map/ppermute | solution.py:18
  95.1 59.9 %collective-permute-start.12 = (bf16[2,128,256]{2,1,0:T(8,128)(2,1)}, bf16[2,128,256]{2,1,0:T(8,128)(2,1)}, u32[]{:S(2)}, u32[]{:S(2)}) collective-permute-start(bf16[2,128,256]{2,1,0:T(8,128)(2,1)} %fusion.68), channel_id=1, source_target_pairs={{0,1},{1,0},{2,3},{3,2},{4,5},{5,4},{6,7},{7,6},{8,9},{9,8},{10,11... | collective-permute-start | bytes 393224 | tf_op jit(solution)/shard_map/ppermute | solution.py:18
  96.7 21.0 %copy-start.18 = (bf16[2,1,16384]{2,0,1:T(2,128)(2,1)S(1)}, bf16[2,1,16384]{2,0,1:T(2,128)(2,1)}, u32[]{:S(2)}) copy-start(bf16[2,1,16384]{2,0,1:T(2,128)(2,1)} %copy.437) | copy-start | bytes 196612
  96.8 21.0 %copy-start.48 = (f32[2]{0:T(128)S(1)}, f32[2]{0:T(128)}, u32[]{:S(2)}) copy-start(f32[2]{0:T(128)} %copy-done.47) | copy-start | bytes 28
  96.8 21.0 %copy-start.59 = (f32[2,1,128]{2,1,0:T(1,128)S(1)}, f32[2,1,128]{2,1,0:T(1,128)}, u32[]{:S(2)}) copy-start(f32[2,1,128]{2,1,0:T(1,128)} %fusion.167) | copy-start | bytes 3076
  151.8 18.5 %collective-permute-start.16 = (bf16[2,1024,256]{2,1,0:T(8,128)(2,1)S(1)}, bf16[2,1024,256]{2,1,0:T(8,128)(2,1)S(1)}, u32[]{:S(2)}, u32[]{:S(2)}) collective-permute-start(bf16[2,1024,256]{2,1,0:T(8,128)(2,1)S(1)} %fusion.36), channel_id=1, source_target_pairs={{0,8},{8,0},{1,9},{9,1},{2,10},{10,2},{3,11},{11,3},{4,12},{12,4},... | collective-permute-start | bytes 3145736 | tf_op jit(solution)/shard_map/ppermute | solution.py:18
  151.9 6.8 %collective-permute-start.14 = (bf16[2,256,256]{2,1,0:T(8,128)(2,1)S(1)}, bf16[2,256,256]{2,1,0:T(8,128)(2,1)S(1)}, u32[]{:S(2)}, u32[]{:S(2)}) collective-permute-start(bf16[2,256,256]{2,1,0:T(8,128)(2,1)S(1)} %fusion.50), channel_id=1, source_target_pairs={{0,2},{2,0},{1,3},{3,1},{4,6},{6,4},{5,7},{7,5},{8,10},{10,8},{9,1... | collective-permute-start | bytes 786440 | tf_op jit(solution)/shard_map/ppermute | solution.py:18
  158.9 12.6 %collective-permute-start.15 = (bf16[2,128,256]{2,1,0:T(8,128)(2,1)S(1)}, bf16[2,128,256]{2,1,0:T(8,128)(2,1)S(1)}, u32[]{:S(2)}, u32[]{:S(2)}) collective-permute-start(bf16[2,128,256]{2,1,0:T(8,128)(2,1)S(1)} %fusion.69), channel_id=1, source_target_pairs={{0,1},{1,0},{2,3},{3,2},{4,5},{5,4},{6,7},{7,6},{8,9},{9,8},{10,11... | collective-permute-start | bytes 393224 | tf_op jit(solution)/shard_map/ppermute | solution.py:18
  170.7 10.4 %collective-permute-start.17 = (bf16[2,512,256]{2,1,0:T(8,128)(2,1)S(1)}, bf16[2,512,256]{2,1,0:T(8,128)(2,1)S(1)}, u32[]{:S(2)}, u32[]{:S(2)}) collective-permute-start(bf16[2,512,256]{2,1,0:T(8,128)(2,1)S(1)} %fusion.43), channel_id=1, source_target_pairs={{0,4},{4,0},{1,5},{5,1},{2,6},{6,2},{3,7},{7,3},{8,12},{12,8},{9,1... | collective-permute-start | bytes 1572872 | tf_op jit(solution)/shard_map/ppermute | solution.py:18
  182.0 67.0 %collective-permute-start.18 = (bf16[2,256,256]{2,1,0:T(8,128)(2,1)}, bf16[2,256,256]{2,1,0:T(8,128)(2,1)}, u32[]{:S(2)}, u32[]{:S(2)}) collective-permute-start(bf16[2,256,256]{2,1,0:T(8,128)(2,1)} %fusion.51), channel_id=1, source_target_pairs={{0,2},{2,0},{1,3},{3,1},{4,6},{6,4},{5,7},{7,5},{8,10},{10,8},{9,1... | collective-permute-start | bytes 786440 | tf_op jit(solution)/shard_map/ppermute | solution.py:18
  186.1 64.6 %copy-start.37 = (f32[256]{0:T(256)S(1)}, f32[256]{0:T(256)}, u32[]{:S(2)}) copy-start(f32[256]{0:T(256)} %param.13) | copy-start | bytes 3076
  250.1 5.2 %collective-permute-start.19 = (bf16[2,128,256]{2,1,0:T(8,128)(2,1)S(1)}, bf16[2,128,256]{2,1,0:T(8,128)(2,1)S(1)}, u32[]{:S(2)}, u32[]{:S(2)}) collective-permute-start(bf16[2,128,256]{2,1,0:T(8,128)(2,1)S(1)} %fusion.70), channel_id=1, source_target_pairs={{0,1},{1,0},{2,3},{3,2},{4,5},{5,4},{6,7},{7,6},{8,9},{9,8},{10,11... | collective-permute-start | bytes 393224 | tf_op jit(solution)/shard_map/ppermute | solution.py:18
  (59 other events, 380.1 us)
